TPU v7x, 512 devices: a whole 4x8x8 slice. The times are simulated.
512 devices in a mesh: blk: 32 (over x, y_hi, core), grp: 16 (over z, y_lo).
Axes of the slice: x: 4, y: 8 (y_hi: 4, y_lo: 2; y = y_hi * 2 + y_lo), z: 8, core: 2. Of those that a mesh axis runs over, the one named last changes fastest.
Arguments:
- amplitudes: bfloat16 [4096, 8, 4, 128], P('blk'), may hold values from -6 to 6
- integrals: bfloat16 [256, 4096, 128], P('grp', 'blk'), may hold values from -0.15625 to 0.15625
- virt_energy: float32 [4096], replicated, may hold values from 0.5 to 4
- pair_energy: float32 [8], replicated, may hold values from -3 to -0.5
- offsets: int32 [32, 4], replicated, may hold values from 0 to 31, as said below
Outputs:
- ladder: float32 [4096, 8, 4, 128], P(('blk', 'grp'))
- new_amplitudes: float32 [4096, 8, 4, 128], P(('blk', 'grp'))
Inputs may be any that keep to these rules, and one draw needn't show every extreme that they name: The 4 offsets of one row tile are different; the first 3 are at most 2, the last is larger than 2.
All inputs are finite; a program needn't handle non-finite values.
Results may differ from a plain program's by a relative error of at most 0.0029.
Values may be sent and summed in bfloat16 or wider, within the bound.
No kernel may reach another device: no remote copies, remote signals or barrier semaphores. Data moves between devices by JAX's collectives and lax.ppermute only.
A program may use at most 64 MiB of HBM per device.

v0:
```python
import jax
import jax.numpy as jnp
from jax import lax
from jax.sharding import PartitionSpec as P


def in_blocks(x, dim, devices):
    before, after = (x.shape[:dim], x.shape[dim + 1 :])
    return jnp.moveaxis(x.reshape(*before, devices, -1, *after), dim, 0)


def sum_at_owner(x, axis, dim):
    devices = lax.axis_size(axis)
    blocks = lax.all_to_all(in_blocks(x, dim, devices), axis, 0, 0, tiled=True)
    return jnp.sum(blocks, axis=0)


def local(amplitudes, integrals, virt_energy, pair_energy, offsets):
    tiles = lax.axis_size("blk")
    tile_index = lax.axis_index("blk")
    group_index = lax.axis_index("grp")
    slab_width = integrals.shape[2]
    aux_local = integrals.shape[0]
    pair_count = amplitudes.shape[1]
    slot_count = amplitudes.shape[2]
    own_offsets = lax.dynamic_slice_in_dim(offsets, tile_index, 1, 0)[0]
    cols = (tile_index - own_offsets) % tiles
    piece = lax.all_gather(integrals, "blk", axis=1, tiled=True)
    count = piece.shape[1] // slab_width
    tile_ids = jnp.arange(count, dtype=jnp.int32)
    onehot = (cols[:, None] == tile_ids[None, :]).astype(jnp.bfloat16)
    pieces = piece.reshape(aux_local, count, slab_width, slab_width)
    chosen = jnp.einsum("sj,qjbd->qsbd", onehot, pieces, preferred_element_type=jnp.float32)
    col_blocks = chosen.astype(jnp.bfloat16)
    flattened_rows = amplitudes.reshape(slab_width, pair_count * slot_count * slab_width)
    rows_per_device = slab_width // lax.axis_size("grp")

    def add_aux(aux, total):
        half_split = jnp.dot(
            integrals[aux], flattened_rows, preferred_element_type=jnp.float32
        ).astype(jnp.bfloat16)
        half_split = half_split.reshape(
            rows_per_device * lax.axis_size("grp"), pair_count, slot_count, slab_width
        )
        return total + jnp.einsum(
            "apsd,sbd->apsb", half_split, col_blocks[aux], preferred_element_type=jnp.float32
        )

    total_start_offset = jnp.zeros(
        (rows_per_device * lax.axis_size("grp"), pair_count, slot_count, slab_width), jnp.float32
    )
    ladder = sum_at_owner(lax.fori_loop(0, aux_local, add_aux, total_start_offset), "grp", 0)
    first_row = group_index * rows_per_device
    old_rows = lax.dynamic_slice_in_dim(amplitudes, first_row, rows_per_device, 0).astype(
        jnp.float32
    )
    row_energy = lax.dynamic_slice_in_dim(
        virt_energy, tile_index * slab_width + first_row, rows_per_device, 0
    )
    table = virt_energy.reshape(tiles, slab_width)
    selector = (cols[:, None] == jnp.arange(tiles, dtype=jnp.int32)[None, :]).astype(jnp.float32)
    col_energy = jnp.dot(selector, table, precision=lax.Precision.HIGHEST)
    denom = (
        row_energy[:, None, None, None]
        + col_energy[None, None, :, :]
        - pair_energy[None, :, None, None]
    )
    new_amplitudes = old_rows - ladder / denom
    return (ladder, new_amplitudes)


def solution(mesh):
    placed = (P("blk", None, None, None), P("grp", "blk", None), P(), P(), P())
    return jax.shard_map(
        local,
        mesh=mesh,
        in_specs=placed,
        out_specs=(P(("blk", "grp"), None, None, None), P(("blk", "grp"), None, None, None)),
        check_vma=False,
    )
```

profile of v0, /device:TPU:6, one launch (start us, length us, event | category | flops | bytes accessed | tf_op | source)
XLA Modules:
  0.0 332.6 jit_solution(4653998717116399375)
XLA Ops:
  7.9 1.8 reshape.51
  10.0 128.8 %all-gather.2.cloned.1.call-done = bf16[16,4096,128]{2,1,0:T(8,128)(2,1)} async-done(((bf16[16,128,128]{2,1,0:T(8,128)(2,1)}), bf16[16,4096,128]{2,1,0:T(8,128)(2,1)}) %all-gather.2.cloned.1.call-update) | async-done | bytes 16777232 | tf_op jit(solution)/shard_map/all_gather | solution.py:28
  138.8 16.6 %convert_bitcast_fusion = bf16[16,4,128,128]{3,1,2,0:T(4,128)(2,1)} fusion(bf16[16,32,128,128]{3,2,1,0:T(8,128)(2,1)} %bitcast.32, s32[4]{0:T(128)S(1)} %and_select_fusion), kind=kOutput, calls=%fused_computation.10 | convolution fusion | flops 68157568 | bytes 18874384 | tf_op jit(solution)/shard_map/sj,qjbd->qsbd/dot_general | solution.py:33
  155.4 105.9 %while.14 = (s32[]{:T(128)}, f32[128,8,4,128]{0,3,1,2:T(8,128)}, bf16[16,4,128,128]{3,1,2,0:T(4,128)(2,1)}, bf16[16,128,128]{2,1,0:T(8,128)(2,1)}, bf16[128,4096]{1,0:T(8,128)(2,1)S(1)}, /*index=5*/s32[]{:T(128)}, s32[]{:T(128)}) while((s32[]{:T(128)}, f32[128,8,4,128]{0,3,1,2:T(8,128)}, bf16[16,4,128,128]{3,1,2,0:T(4,128)(2,1)}, ...), condition=%wide.region_1.2_spmd.clone, body=%wide.region_0.1_spmd.clone.sunk | while | flops 270008320 | bytes 9863271 | solution.py:52
  156.4 1.2 convolution_convert_fusion.2
  158.3 2.2 bitcast_add_fusion.2
  163.4 3.8 %bitcast_add_fusion.2 = f32[128,8,4,128]{0,3,1,2:T(8,128)} fusion(f32[128,8,4,128]{0,3,1,2:T(8,128)} %get-tuple-element.181, bf16[128,8,4,128]{3,2,1,0:T(4,128)(2,1)S(1)} %reshape.59, pred[]{:T(512)S(6)} %compare.7, bf16[1,4,128,128]{3,1,2,0:T(4,128)(2,1)S(1)} %constant_dynamic-slice_fusion.3), kind=kOutput, calls=%fused_computation.1.clone.1 | convolution fusion | flops 135266304 | bytes 5373953 | tf_op jit(solution)/shard_map/while/body/eval_jaxpr/apsd,sbd->apsb/dot_general | solution.py:45
  170.2 3.8 %bitcast_add_fusion.2 = f32[128,8,4,128]{0,3,1,2:T(8,128)} fusion(f32[128,8,4,128]{0,3,1,2:T(8,128)} %get-tuple-element.181, bf16[128,8,4,128]{3,2,1,0:T(4,128)(2,1)S(1)} %reshape.59, pred[]{:T(512)S(6)} %compare.7, bf16[1,4,128,128]{3,1,2,0:T(4,128)(2,1)S(1)} %constant_dynamic-slice_fusion.3), kind=kOutput, calls=%fused_computation.1.clone.1 | convolution fusion | flops 135266304 | bytes 5373953 | tf_op jit(solution)/shard_map/while/body/eval_jaxpr/apsd,sbd->apsb/dot_general | solution.py:45
  176.9 3.8 %bitcast_add_fusion.2 = f32[128,8,4,128]{0,3,1,2:T(8,128)} fusion(f32[128,8,4,128]{0,3,1,2:T(8,128)} %get-tuple-element.181, bf16[128,8,4,128]{3,2,1,0:T(4,128)(2,1)S(1)} %reshape.59, pred[]{:T(512)S(6)} %compare.7, bf16[1,4,128,128]{3,1,2,0:T(4,128)(2,1)S(1)} %constant_dynamic-slice_fusion.3), kind=kOutput, calls=%fused_computation.1.clone.1 | convolution fusion | flops 135266304 | bytes 5373953 | tf_op jit(solution)/shard_map/while/body/eval_jaxpr/apsd,sbd->apsb/dot_general | solution.py:45
  183.6 3.8 %bitcast_add_fusion.2 = f32[128,8,4,128]{0,3,1,2:T(8,128)} fusion(f32[128,8,4,128]{0,3,1,2:T(8,128)} %get-tuple-element.181, bf16[128,8,4,128]{3,2,1,0:T(4,128)(2,1)S(1)} %reshape.59, pred[]{:T(512)S(6)} %compare.7, bf16[1,4,128,128]{3,1,2,0:T(4,128)(2,1)S(1)} %constant_dynamic-slice_fusion.3), kind=kOutput, calls=%fused_computation.1.clone.1 | convolution fusion | flops 135266304 | bytes 5373953 | tf_op jit(solution)/shard_map/while/body/eval_jaxpr/apsd,sbd->apsb/dot_general | solution.py:45
  190.3 3.8 %bitcast_add_fusion.2 = f32[128,8,4,128]{0,3,1,2:T(8,128)} fusion(f32[128,8,4,128]{0,3,1,2:T(8,128)} %get-tuple-element.181, bf16[128,8,4,128]{3,2,1,0:T(4,128)(2,1)S(1)} %reshape.59, pred[]{:T(512)S(6)} %compare.7, bf16[1,4,128,128]{3,1,2,0:T(4,128)(2,1)S(1)} %constant_dynamic-slice_fusion.3), kind=kOutput, calls=%fused_computation.1.clone.1 | convolution fusion | flops 135266304 | bytes 5373953 | tf_op jit(solution)/shard_map/while/body/eval_jaxpr/apsd,sbd->apsb/dot_general | solution.py:45
  197.0 3.8 %bitcast_add_fusion.2 = f32[128,8,4,128]{0,3,1,2:T(8,128)} fusion(f32[128,8,4,128]{0,3,1,2:T(8,128)} %get-tuple-element.181, bf16[128,8,4,128]{3,2,1,0:T(4,128)(2,1)S(1)} %reshape.59, pred[]{:T(512)S(6)} %compare.7, bf16[1,4,128,128]{3,1,2,0:T(4,128)(2,1)S(1)} %constant_dynamic-slice_fusion.3), kind=kOutput, calls=%fused_computation.1.clone.1 | convolution fusion | flops 135266304 | bytes 5373953 | tf_op jit(solution)/shard_map/while/body/eval_jaxpr/apsd,sbd->apsb/dot_general | solution.py:45
  203.7 3.8 %bitcast_add_fusion.2 = f32[128,8,4,128]{0,3,1,2:T(8,128)} fusion(f32[128,8,4,128]{0,3,1,2:T(8,128)} %get-tuple-element.181, bf16[128,8,4,128]{3,2,1,0:T(4,128)(2,1)S(1)} %reshape.59, pred[]{:T(512)S(6)} %compare.7, bf16[1,4,128,128]{3,1,2,0:T(4,128)(2,1)S(1)} %constant_dynamic-slice_fusion.3), kind=kOutput, calls=%fused_computation.1.clone.1 | convolution fusion | flops 135266304 | bytes 5373953 | tf_op jit(solution)/shard_map/while/body/eval_jaxpr/apsd,sbd->apsb/dot_general | solution.py:45
  210.5 3.8 %bitcast_add_fusion.2 = f32[128,8,4,128]{0,3,1,2:T(8,128)} fusion(f32[128,8,4,128]{0,3,1,2:T(8,128)} %get-tuple-element.181, bf16[128,8,4,128]{3,2,1,0:T(4,128)(2,1)S(1)} %reshape.59, pred[]{:T(512)S(6)} %compare.7, bf16[1,4,128,128]{3,1,2,0:T(4,128)(2,1)S(1)} %constant_dynamic-slice_fusion.3), kind=kOutput, calls=%fused_computation.1.clone.1 | convolution fusion | flops 135266304 | bytes 5373953 | tf_op jit(solution)/shard_map/while/body/eval_jaxpr/apsd,sbd->apsb/dot_general | solution.py:45
  217.2 3.8 %bitcast_add_fusion.2 = f32[128,8,4,128]{0,3,1,2:T(8,128)} fusion(f32[128,8,4,128]{0,3,1,2:T(8,128)} %get-tuple-element.181, bf16[128,8,4,128]{3,2,1,0:T(4,128)(2,1)S(1)} %reshape.59, pred[]{:T(512)S(6)} %compare.7, bf16[1,4,128,128]{3,1,2,0:T(4,128)(2,1)S(1)} %constant_dynamic-slice_fusion.3), kind=kOutput, calls=%fused_computation.1.clone.1 | convolution fusion | flops 135266304 | bytes 5373953 | tf_op jit(solution)/shard_map/while/body/eval_jaxpr/apsd,sbd->apsb/dot_general | solution.py:45
  223.9 3.8 %bitcast_add_fusion.2 = f32[128,8,4,128]{0,3,1,2:T(8,128)} fusion(f32[128,8,4,128]{0,3,1,2:T(8,128)} %get-tuple-element.181, bf16[128,8,4,128]{3,2,1,0:T(4,128)(2,1)S(1)} %reshape.59, pred[]{:T(512)S(6)} %compare.7, bf16[1,4,128,128]{3,1,2,0:T(4,128)(2,1)S(1)} %constant_dynamic-slice_fusion.3), kind=kOutput, calls=%fused_computation.1.clone.1 | convolution fusion | flops 135266304 | bytes 5373953 | tf_op jit(solution)/shard_map/while/body/eval_jaxpr/apsd,sbd->apsb/dot_general | solution.py:45
  230.6 3.8 %bitcast_add_fusion.2 = f32[128,8,4,128]{0,3,1,2:T(8,128)} fusion(f32[128,8,4,128]{0,3,1,2:T(8,128)} %get-tuple-element.181, bf16[128,8,4,128]{3,2,1,0:T(4,128)(2,1)S(1)} %reshape.59, pred[]{:T(512)S(6)} %compare.7, bf16[1,4,128,128]{3,1,2,0:T(4,128)(2,1)S(1)} %constant_dynamic-slice_fusion.3), kind=kOutput, calls=%fused_computation.1.clone.1 | convolution fusion | flops 135266304 | bytes 5373953 | tf_op jit(solution)/shard_map/while/body/eval_jaxpr/apsd,sbd->apsb/dot_general | solution.py:45
  237.3 3.8 %bitcast_add_fusion.2 = f32[128,8,4,128]{0,3,1,2:T(8,128)} fusion(f32[128,8,4,128]{0,3,1,2:T(8,128)} %get-tuple-element.181, bf16[128,8,4,128]{3,2,1,0:T(4,128)(2,1)S(1)} %reshape.59, pred[]{:T(512)S(6)} %compare.7, bf16[1,4,128,128]{3,1,2,0:T(4,128)(2,1)S(1)} %constant_dynamic-slice_fusion.3), kind=kOutput, calls=%fused_computation.1.clone.1 | convolution fusion | flops 135266304 | bytes 5373953 | tf_op jit(solution)/shard_map/while/body/eval_jaxpr/apsd,sbd->apsb/dot_general | solution.py:45
  244.0 3.8 %bitcast_add_fusion.2 = f32[128,8,4,128]{0,3,1,2:T(8,128)} fusion(f32[128,8,4,128]{0,3,1,2:T(8,128)} %get-tuple-element.181, bf16[128,8,4,128]{3,2,1,0:T(4,128)(2,1)S(1)} %reshape.59, pred[]{:T(512)S(6)} %compare.7, bf16[1,4,128,128]{3,1,2,0:T(4,128)(2,1)S(1)} %constant_dynamic-slice_fusion.3), kind=kOutput, calls=%fused_computation.1.clone.1 | convolution fusion | flops 135266304 | bytes 5373953 | tf_op jit(solution)/shard_map/while/body/eval_jaxpr/apsd,sbd->apsb/dot_general | solution.py:45
  250.8 3.8 %bitcast_add_fusion.2 = f32[128,8,4,128]{0,3,1,2:T(8,128)} fusion(f32[128,8,4,128]{0,3,1,2:T(8,128)} %get-tuple-element.181, bf16[128,8,4,128]{3,2,1,0:T(4,128)(2,1)S(1)} %reshape.59, pred[]{:T(512)S(6)} %compare.7, bf16[1,4,128,128]{3,1,2,0:T(4,128)(2,1)S(1)} %constant_dynamic-slice_fusion.3), kind=kOutput, calls=%fused_computation.1.clone.1 | convolution fusion | flops 135266304 | bytes 5373953 | tf_op jit(solution)/shard_map/while/body/eval_jaxpr/apsd,sbd->apsb/dot_general | solution.py:45
  257.5 3.8 %bitcast_add_fusion.2 = f32[128,8,4,128]{0,3,1,2:T(8,128)} fusion(f32[128,8,4,128]{0,3,1,2:T(8,128)} %get-tuple-element.181, bf16[128,8,4,128]{3,2,1,0:T(4,128)(2,1)S(1)} %reshape.59, pred[]{:T(512)S(6)} %compare.7, bf16[1,4,128,128]{3,1,2,0:T(4,128)(2,1)S(1)} %constant_dynamic-slice_fusion.3), kind=kOutput, calls=%fused_computation.1.clone.1 | convolution fusion | flops 135266304 | bytes 5373953 | tf_op jit(solution)/shard_map/while/body/eval_jaxpr/apsd,sbd->apsb/dot_general | solution.py:45
  261.3 3.1 copy.16
  264.4 8.6 %all-to-all-start = ((f32[16,8,8,4,128]{4,2,3,1,0:T(8,128)}), f32[16,8,8,4,128]{4,2,3,1,0:T(8,128)S(1)}, u32[]{:S(2)}, u32[]{:S(2)}) async-start(f32[16,8,8,4,128]{4,2,3,1,0:T(8,128)} %bitcast.33), calls=%async_computation | async-start | bytes 4194304 | tf_op jit(solution)/shard_map/all_to_all | solution.py:14
  274.2 49.9 %all-to-all-done = f32[16,8,8,4,128]{4,2,3,1,0:T(8,128)S(1)} async-done(((f32[16,8,8,4,128]{4,2,3,1,0:T(8,128)}), f32[16,8,8,4,128]{4,2,3,1,0:T(8,128)S(1)}, u32[]{:S(2)}, u32[]{:S(2)}) %all-to-all-start) | async-done | bytes 2097184 | tf_op jit(solution)/shard_map/all_to_all | solution.py:14
  (66 shorter events, 49.0 us)
Async XLA Ops:
  7.2 2.6 copy-start
  7.2 131.6 %all-gather.2.cloned.1.call-start = ((), (), s32[]{:S(2)}) async-start(), calls=%async_computation.1 | async-start | bytes 17301504 | tf_op jit(solution)/shard_map/all_gather | solution.py:28
  264.4 8.6 %copy-start.2 = (f32[4096]{0:T(1024)S(1)}, f32[4096]{0:T(1024)}, u32[]{:S(2)}) copy-start(f32[4096]{0:T(1024)} %param.9) | copy-start | bytes 49156
  264.4 59.8 %all-to-all-start = ((f32[16,8,8,4,128]{4,2,3,1,0:T(8,128)}), f32[16,8,8,4,128]{4,2,3,1,0:T(8,128)S(1)}, u32[]{:S(2)}, u32[]{:S(2)}) async-start(f32[16,8,8,4,128]{4,2,3,1,0:T(8,128)} %bitcast.33), calls=%async_computation | async-start | bytes 4194304 | tf_op jit(solution)/shard_map/all_to_all | solution.py:14
  273.0 52.0 %copy-start.1 = (f32[8]{0:T(128)S(1)}, f32[8]{0:T(128)}, u32[]{:S(2)}) copy-start(f32[8]{0:T(128)} %param.10) | copy-start | bytes 100
Sparse Core Ops, SparseCore 0:
  11.2 127.5 all-gather.1
where the time goes:
time: 335 us; the launch traced here: 333 us
  waiting for transfers between devices  179 us (53%)
  matrix products  94.9 us (28%)
  local copies, waits for them, and re-layouts  34.7 us (10%)
  between operations  14.1 us (4%)
  starting transfers between devices  8.64 us (3%)
    all_gather x1, waiting for transfers between devices, local(): piece = lax.all_gather(integrals, 'blk', axis=1, tiled=True)  129 us
    dot_general x16, matrix products, add_aux(): jnp.einsum('apsd,sbd->apsb', half_split, col_blocks[aux], preferred_eleme...  59.2 us
    all_to_all x1, waiting for transfers between devices, sum_at_owner(): blocks = lax.all_to_all(in_blocks(x, dim, devices), axis, 0, 0, tiled=True)  49.9 us
    dot_general x16, matrix products, add_aux(): jnp.dot(integrals[aux], flattened_rows, preferred_element_type=jnp.float32)  18.9 us
    dot_general x1, matrix products, local(): jnp.einsum('sj,qjbd->qsbd', onehot, pieces, preferred_element_type=jnp.fl...  16.6 us
    dynamic_slice x16, local copies, waits for them, and re-layouts, add_aux(): col_blocks[aux]  15.2 us
    reshape x16, local copies, waits for them, and re-layouts, add_aux(): half_split.reshape(rows_per_device * lax.axis_size('grp'), pair_count, sl...  12.2 us
    all_to_all x1, starting transfers between devices, sum_at_owner(): blocks = lax.all_to_all(in_blocks(x, dim, devices), axis, 0, 0, tiled=True)  8.6 us
  transfers between devices with their start and end apart: 2, of which 2 were waited for; matrix products, arithmetic and copies ran while one was open for 1% of the time, Pallas kernels for 0%

commit v1 on v0

v1 whole, which is shorter than its diff:
```python
import functools

import jax
import jax.numpy as jnp
from jax import lax
from jax.experimental import pallas as pl
from jax.experimental.pallas import tpu as pltpu
from jax.sharding import PartitionSpec as P


QUAD = 4


def pick_kernel(index_ref, source_ref, out_ref, sem):
    def copy(row):
        return pltpu.make_async_copy(source_ref.at[index_ref[row]], out_ref.at[row], sem.at[row])

    rows = out_ref.shape[0]
    for row in range(rows):
        copy(row).start()
    for row in range(rows):
        copy(row).wait()


def pick_rows(source, index):
    return pl.pallas_call(
        pick_kernel,
        out_shape=jax.ShapeDtypeStruct(source.shape, source.dtype),
        in_specs=[
            pl.BlockSpec(memory_space=pltpu.SMEM),
            pl.BlockSpec(memory_space=pl.ANY),
        ],
        out_specs=pl.BlockSpec(memory_space=pltpu.VMEM),
        scratch_shapes=[pltpu.SemaphoreType.DMA((source.shape[0],))],
        cost_estimate=pl.CostEstimate(flops=0, transcendentals=0, bytes_accessed=4 * source.size),
        name="pick_rows",
    )(index, source)


def ladder_kernel(tiles, amps, rows_from, cols_from, job_ref, *refs):
    tile_refs, amp_refs = refs[:tiles], refs[tiles : tiles + amps]
    head_refs, (out_ref, *scratch) = refs[tiles + amps : -6], refs[-6:]
    own_ref, cols_ref, amp_ref, half_ref, total_ref = scratch
    aux, width = tile_refs[0].shape[0], tile_refs[0].shape[1]
    pairs, columns = half_ref.shape[0], total_ref.shape[0]
    head = sum(ref.shape[1] for ref in head_refs)
    jobs = (out_ref.shape[1] - head) // columns
    for ref in head_refs:
        out_ref[:, :head] = ref[...]

    @pl.loop(0, jobs)
    def _(job):
        for number in rows_from:

            @pl.when(job_ref[0, job] == number)
            def _():
                own_ref[...] = tile_refs[number][...]

        for number in cols_from:

            @pl.when(job_ref[1, job] == number)
            def _():
                for q in range(aux):
                    cols_ref[q // QUAD, :, (q % QUAD) * width : (q % QUAD + 1) * width] = tile_refs[
                        number
                    ][q]

        for number in range(amps):

            @pl.when(job_ref[2, job] == number)
            def _():
                amp_ref[...] = amp_refs[number][job_ref[3, job]]

        total_ref[...] = jnp.zeros_like(total_ref)

        @pl.loop(0, aux // QUAD)
        def _(step):
            rows = own_ref[pl.ds(step * QUAD, QUAD)].reshape(QUAD * width, width)
            for p in range(0, pairs, 2):
                half = jnp.dot(
                    rows,
                    amp_ref[:, p * width : (p + 2) * width],
                    preferred_element_type=jnp.float32,
                ).astype(jnp.bfloat16)
                for k in range(2):
                    for q in range(QUAD):
                        half_ref[p + k, :, q * width : (q + 1) * width] = half[
                            q * width : (q + 1) * width, k * width : (k + 1) * width
                        ]
            total_ref[...] += lax.dot_general(
                half_ref[...].reshape(pairs * width, QUAD * width),
                cols_ref[step],
                (((1,), (1,)), ((), ())),
                preferred_element_type=jnp.float32,
            )

        for p in range(pairs):
            start = pl.multiple_of(head + job * columns + p * width, width)
            out_ref[:, pl.ds(start, width)] = total_ref[p * width : (p + 1) * width, :].astype(
                jnp.bfloat16
            )


def partial_ladder(jobs, tiles, amps, heads, rows_from, cols_from):
    aux, width, _ = tiles[0].shape
    columns = amps[0].shape[2]
    pairs, count = columns // width, jobs.shape[1]
    arrays = [*tiles, *amps, *heads]
    total = sum(head.shape[1] for head in heads) + count * columns
    return pl.pallas_call(
        functools.partial(ladder_kernel, len(tiles), len(amps), rows_from, cols_from),
        out_shape=jax.ShapeDtypeStruct((width, total), jnp.bfloat16),
        in_specs=[pl.BlockSpec(memory_space=pltpu.SMEM)]
        + [pl.BlockSpec(memory_space=pltpu.VMEM)] * len(arrays),
        out_specs=pl.BlockSpec(memory_space=pltpu.VMEM),
        scratch_shapes=[
            pltpu.VMEM((aux, width, width), jnp.bfloat16),
            pltpu.VMEM((aux // QUAD, width, QUAD * width), jnp.bfloat16),
            pltpu.VMEM((width, columns), jnp.bfloat16),
            pltpu.VMEM((pairs, width, QUAD * width), jnp.bfloat16),
            pltpu.VMEM((columns, width), jnp.float32),
        ],
        cost_estimate=pl.CostEstimate(
            flops=4 * count * aux * width * width * columns,
            transcendentals=0,
            bytes_accessed=2 * sum(a.size for a in arrays) + 2 * width * total,
        ),
        compiler_params=pltpu.CompilerParams(vmem_limit_bytes=32 * 1024 * 1024),
    )(jobs, *arrays)


def local(amplitudes, integrals, virt_energy, pair_energy, offsets):
    tiles = lax.axis_size("blk")
    groups = lax.axis_size("grp")
    tile_index = lax.axis_index("blk")
    group_index = lax.axis_index("grp")
    aux, width, _ = integrals.shape
    pairs, slots = amplitudes.shape[1], amplitudes.shape[2]
    near = slots - 1
    rows = width // groups
    numbers = jnp.arange(tiles, dtype=jnp.int32)
    odd = tile_index % 2
    even_tiles, odd_tiles = range(0, tiles, 2), range(1, tiles, 2)

    own_offsets = lax.dynamic_slice_in_dim(offsets, tile_index, 1, 0)[0]
    slot_of = jnp.argmax(
        own_offsets[None, :near] == jnp.arange(near, dtype=jnp.int32)[:, None], axis=1
    ).astype(jnp.int32)

    spread = lax.all_to_all(
        integrals.reshape(tiles, aux * width // tiles, width), "blk", 0, 0, tiled=True
    )
    hop = [(i, (i + 2) % tiles) for i in odd_tiles] + [(i, (i - 2) % tiles) for i in even_tiles]
    across = lax.ppermute(integrals, "blk", hop)
    beside = lax.ppermute(integrals, "blk", [(i, i + 1) for i in even_tiles])
    amps = amplitudes.transpose(2, 0, 1, 3).reshape(slots, width, pairs * width)
    amps_above = lax.ppermute(
        lax.dynamic_slice_in_dim(amps, slot_of[2], 1, 0),
        "blk",
        [(i, (i - 2) % tiles) for i in even_tiles],
    )
    far_index = (numbers - offsets[:, near]) % tiles
    picked = pick_rows(spread, far_index)
    far = lax.all_to_all(picked, "blk", 0, 0, tiled=True).reshape(integrals.shape)
    before = lax.ppermute(across, "blk", [(i, i - 1) for i in odd_tiles])

    zero, one = jnp.int32(0), jnp.int32(1)

    jobs = jnp.stack([zero, zero, zero, slot_of[0]]).reshape(4, 1)
    piece = partial_ladder(jobs, [integrals], [amps], [], (0,), (0,))
    jobs = jnp.stack(
        [
            jnp.stack([zero, 1 - odd]),
            jnp.stack([3 - odd, odd]),
            jnp.stack([zero, 1 - odd]),
            jnp.stack([slot_of[1], odd * slot_of[2]]),
        ]
    ).astype(jnp.int32)
    piece = partial_ladder(
        jobs, [integrals, across, beside, before], [amps, amps_above], [piece], (0, 1), (0, 1, 2, 3)
    )
    jobs = jnp.stack([zero, one, zero, jnp.int32(near)]).reshape(4, 1)
    piece = partial_ladder(jobs, [integrals, far], [amps], [piece], (0,), (1,))
    sums = lax.all_to_all(piece.reshape(groups, rows, -1), "grp", 0, 0, tiled=True)
    sums = jnp.sum(sums.astype(jnp.float32), axis=0).reshape(rows, slots, pairs, width)
    near_sum, far_sum = sums[:, :near], sums[:, near]

    third = near_sum[:, 2]
    carried = lax.ppermute(third, "blk", [(i, (i + 2) % tiles) for i in even_tiles])
    third = jnp.where(odd == 1, third, carried)
    parts = [
        jnp.where(
            own_offsets[s] == 0, near_sum[:, 0], jnp.where(own_offsets[s] == 1, near_sum[:, 1], third)
        )
        for s in range(near)
    ]
    ladder = jnp.stack(parts + [far_sum], axis=2)

    first_row = group_index * rows
    old_rows = lax.dynamic_slice_in_dim(amplitudes, first_row, rows, 0).astype(jnp.float32)
    row_energy = lax.dynamic_slice_in_dim(virt_energy, tile_index * width + first_row, rows, 0)
    cols = (tile_index - own_offsets) % tiles
    table = virt_energy.reshape(tiles, width)
    chosen = cols[:, None, None] == numbers[None, :, None]
    col_energy = jnp.sum(jnp.where(chosen, table[None], 0.0), axis=1)
    denom = (
        row_energy[:, None, None, None]
        + col_energy[None, None, :, :]
        - pair_energy[None, :, None, None]
    )
    return (ladder, old_rows - ladder / denom)


def solution(mesh):
    placed = (P("blk", None, None, None), P("grp", "blk", None), P(), P(), P())
    return jax.shard_map(
        local,
        mesh=mesh,
        in_specs=placed,
        out_specs=(P(("blk", "grp"), None, None, None), P(("blk", "grp"), None, None, None)),
        check_vma=False,
    )
```

time: 335 us -> 132 us (0.39)
  the two profiles are of different devices: /device:TPU:6 before, /device:TPU:8 now
where the time goes in v1:
time: 132 us; the launch traced here: 131 us
  starting transfers between devices  52.9 us (40%)
  waiting for transfers between devices  37.4 us (28%)
  Pallas kernels  18.2 us (14%)
  local copies, waits for them, and re-layouts  11.7 us (9%)
  between operations  7.3 us (6%)
  other arithmetic  3.38 us (3%)
    all_to_all x1, waiting for transfers between devices, local(): lax.all_to_all(piece.reshape(groups, rows, -1), 'grp', 0, 0, tiled=True)  26.1 us
    all_to_all x1, starting transfers between devices, local(): lax.all_to_all(piece.reshape(groups, rows, -1), 'grp', 0, 0, tiled=True)  19.2 us
    pallas_call x3, Pallas kernels, partial_ladder(): pl.pallas_call(functools.partial(ladder_kernel, len(tiles), len(amps), ro...  15.3 us
    all_to_all x1, starting transfers between devices, local(): lax.all_to_all(integrals.reshape(tiles, aux * width // tiles, width), 'bl...  9.2 us
    ppermute x1, starting transfers between devices, local(): across = lax.ppermute(integrals, 'blk', hop)  8 us
    ppermute x1, starting transfers between devices, local(): lax.ppermute(lax.dynamic_slice_in_dim(amps, slot_of[2], 1, 0), 'blk', [(i...  7.99 us
    all_to_all x1, waiting for transfers between devices, local(): lax.all_to_all(integrals.reshape(tiles, aux * width // tiles, width), 'bl...  7.08 us
    unnamed x25, local copies, waits for them, and re-layouts  5.97 us
  transfers between devices with their start and end apart: 8, of which 3 were waited for; matrix products, arithmetic and copies ran while one was open for 7% of the time, Pallas kernels for 10%

profile of v1, /device:TPU:8, one launch (start us, length us, event | category | flops | bytes accessed | tf_op | source)
XLA Modules:
  0.0 130.8 jit_solution(11539990641026970684)
XLA Ops:
  0.6 9.2 %all-to-all-start = ((bf16[32,64,128]{2,1,0:T(8,128)(2,1)}), bf16[32,64,128]{2,1,0:T(8,128)(2,1)S(1)}, u32[]{:S(2)}, u32[]{:S(2)}) async-start(bf16[32,64,128]{2,1,0:T(8,128)(2,1)} %bitcast.70), calls=%async_computation | async-start | bytes 1048576 | tf_op jit(solution)/shard_map/all_to_all | solution.py:150
  9.9 8.0 %collective-permute-start = (bf16[16,128,128]{2,1,0:T(8,128)(2,1)S(1)}, bf16[16,128,128]{2,1,0:T(8,128)(2,1)S(1)}, u32[]{:S(2)}, u32[]{:S(2)}) collective-permute-start(bf16[16,128,128]{2,1,0:T(8,128)(2,1)S(1)} %copy-done), channel_id=1, source_target_pairs={{16,48},{48,80},{80,112},{112,144},{144,176},{176,208},{208,240},{... | collective-permute-start | bytes 1572872 | tf_op jit(solution)/shard_map/ppermute | solution.py:154
  17.9 1.3 %collective-permute-start.1 = (bf16[16,128,128]{2,1,0:T(8,128)(2,1)S(1)}, bf16[16,128,128]{2,1,0:T(8,128)(2,1)S(1)}, u32[]{:S(2)}, u32[]{:S(2)}) collective-permute-start(bf16[16,128,128]{2,1,0:T(8,128)(2,1)S(1)} %copy-done), channel_id=1, source_target_pairs={{0,16},{32,48},{64,80},{96,112},{128,144},{160,176},{192,208},{224... | collective-permute-start | bytes 1572872 | tf_op jit(solution)/shard_map/ppermute | solution.py:155
  20.1 7.1 %all-to-all-done.source_ref = bf16[32,64,128]{2,1,0:T(8,128)(2,1)S(1)} async-done(((bf16[32,64,128]{2,1,0:T(8,128)(2,1)}), bf16[32,64,128]{2,1,0:T(8,128)(2,1)S(1)}, u32[]{:S(2)}, u32[]{:S(2)}) %all-to-all-start) | async-done | bytes 524320 | tf_op jit(solution)/shard_map/all_to_all | solution.py:150
  27.1 0.8 copy-done.6
  27.9 2.9 %pick_rows.1 = bf16[32,64,128]{2,1,0:T(8,128)(2,1)} custom-call(s32[32]{0:T(128)} %and_select_fusion.1.index_ref, bf16[32,64,128]{2,1,0:T(8,128)(2,1)} %copy-done.6), custom_call_target="tpu_custom_call" | custom-call | bytes 1048576 | tf_op jit(solution)/shard_map/pick_rows/pallas_call | solution.py:26
  30.8 3.9 %all-to-all-start.1 = ((bf16[32,64,128]{2,1,0:T(8,128)(2,1)}), bf16[32,64,128]{2,1,0:T(8,128)(2,1)S(1)}, u32[]{:S(2)}, u32[]{:S(2)}) async-start(bf16[32,64,128]{2,1,0:T(8,128)(2,1)} %pick_rows.1), calls=%async_computation.1 | async-start | bytes 1048576 | tf_op jit(solution)/shard_map/all_to_all | solution.py:164
  37.4 1.1 copy.20
  38.5 1.5 %reshape.96.refs_1_.refs_4_.refs_2_ = bf16[4,128,1024]{2,1,0:T(8,128)(2,1)S(1)} reshape(bf16[4,128,8,128]{3,2,1,0:T(8,128)(2,1)} %copy.20) | data formatting | bytes 2097152 | tf_op jit(solution)/shard_map/reshape | solution.py:156
  41.4 8.0 %collective-permute-start.3 = (bf16[1,128,1024]{2,1,0:T(8,128)(2,1)}, bf16[1,128,1024]{2,1,0:T(8,128)(2,1)S(1)}, u32[]{:S(2)}, u32[]{:S(2)}) collective-permute-start(bf16[1,128,1024]{2,1,0:T(8,128)(2,1)} %constant_dynamic-slice_fusion.1), channel_id=1, source_target_pairs={{0,480},{32,0},{64,32},{96,64},{128,96},{160,128},{192,160},{224,1... | collective-permute-start | bytes 786440 | tf_op jit(solution)/shard_map/ppermute | solution.py:157
  50.1 1.3 collective-permute-start.2
  53.0 3.5 %shard_map.68.refs_6_ = bf16[128,1024]{1,0:T(8,128)(2,1)S(1)} custom-call(s32[4,1]{1,0:T(4,128)S(1)} %copy.21.job_ref, bf16[16,128,128]{2,1,0:T(8,128)(2,1)S(1)} %copy-done, bf16[4,128,1024]{2,1,0:T(8,128)(2,1)S(1)} %reshape.96.refs_1_.refs_4_.refs_2_), custom_call_target="tpu_custom_call" | custom-call | flops 1073741824 | bytes 1835008 | tf_op jit(solution)/shard_map/pallas_call | solution.py:110
  57.4 0.9 copy-done.5
  58.3 7.1 %shard_map.69.refs_3_ = bf16[128,3072]{1,0:T(8,128)(2,1)S(1)} custom-call(s32[4,2]{1,0:T(4,128)S(1)} %pad_add_fusion.job_ref, bf16[16,128,128]{2,1,0:T(8,128)(2,1)S(1)} %copy-done, bf16[16,128,128]{2,1,0:T(8,128)(2,1)S(1)} %collective-permute-done.refs_1_, bf16[16,128,128]{2,1,0:T(8,128)(2,1)S(1)} %collective-permute-done.1.refs_2_, ...), custom_call_target="tpu_custom_call" | custom-call | flops 2147483648 | bytes 4456448 | tf_op jit(solution)/shard_map/pallas_call | solution.py:110
  65.4 0.9 copy-done.2
  66.3 1.1 copy-done.3
  67.5 4.6 %shard_map.70 = bf16[128,4096]{1,0:T(8,128)(2,1)} custom-call(s32[4,1]{1,0:T(4,128)S(1)} %copy-done.1, bf16[16,128,128]{2,1,0:T(8,128)(2,1)S(1)} %copy-done, bf16[16,128,128]{2,1,0:T(8,128)(2,1)S(1)} %bitcast.71, bf16[4,128,1024]{2,1,0:T(8,128)(2,1)S(1)} %reshape.96.refs_1_.refs_4_.refs_2_, bf16[128,3072]{1,0:T(8,128)(2,1)S(1)} %copy-done.3), custom_call_target="tpu_custom_call" | custom-call | flops 1073741824 | bytes 3932160 | tf_op jit(solution)/shard_map/pallas_call | solution.py:110
  72.0 19.2 %all-to-all-start.2 = ((bf16[16,8,4096]{2,1,0:T(8,128)(2,1)}), bf16[16,8,4096]{2,1,0:T(8,128)(2,1)S(1)}, u32[]{:S(2)}, u32[]{:S(2)}) async-start(bf16[16,8,4096]{2,1,0:T(8,128)(2,1)} %bitcast.14), calls=%async_computation.2 | async-start | bytes 2097152 | tf_op jit(solution)/shard_map/all_to_all | solution.py:184
  91.4 0.9 constant_dynamic-slice_fusion
  92.5 26.1 %all-to-all-done.2 = bf16[16,8,4096]{2,1,0:T(8,128)(2,1)S(1)} async-done(((bf16[16,8,4096]{2,1,0:T(8,128)(2,1)}), bf16[16,8,4096]{2,1,0:T(8,128)(2,1)S(1)}, u32[]{:S(2)}, u32[]{:S(2)}) %all-to-all-start.2) | async-done | bytes 1048608 | tf_op jit(solution)/shard_map/all_to_all | solution.py:184
  118.8 1.9 %collective-permute-start.4 = (f32[8,8,128]{2,1,0:T(8,128)S(1)}, f32[8,8,128]{2,1,0:T(8,128)S(1)}, u32[]{:S(2)}, u32[]{:S(2)}) collective-permute-start(f32[8,8,128]{2,1,0:T(8,128)S(1)} %get-tuple-element.16), channel_id=1, source_target_pairs={{0,32},{32,64},{64,96},{96,128},{128,160},{160,192},{192,224},{224... | collective-permute-start | bytes 98312 | tf_op jit(solution)/shard_map/ppermute | solution.py:189
  125.0 4.2 %collective-permute-done.4 = f32[8,8,128]{2,1,0:T(8,128)S(1)} collective-permute-done((f32[8,8,128]{2,1,0:T(8,128)S(1)}, f32[8,8,128]{2,1,0:T(8,128)S(1)}, u32[]{:S(2)}, u32[]{:S(2)}) %collective-permute-start.4) | collective-permute-done | bytes 32800 | tf_op jit(solution)/shard_map/ppermute | solution.py:189
  129.3 0.7 copy.26
  130.1 0.7 copy.27
  (47 shorter events, 6.4 us)
Async XLA Ops:
  0.6 9.2 %copy-start = (bf16[16,128,128]{2,1,0:T(8,128)(2,1)S(1)}, bf16[16,128,128]{2,1,0:T(8,128)(2,1)}, u32[]{:S(2)}) copy-start(bf16[16,128,128]{2,1,0:T(8,128)(2,1)} %refs_0_.5) | copy-start | bytes 1572868
  0.6 18.6 %copy-start.9 = (s32[32,4]{0,1:T(4,128)S(1)}, s32[32,4]{0,1:T(4,128)}, u32[]{:S(2)}) copy-start(s32[32,4]{0,1:T(4,128)} %param.9) | copy-start | bytes 1540
  0.6 26.5 %all-to-all-start = ((bf16[32,64,128]{2,1,0:T(8,128)(2,1)}), bf16[32,64,128]{2,1,0:T(8,128)(2,1)S(1)}, u32[]{:S(2)}, u32[]{:S(2)}) async-start(bf16[32,64,128]{2,1,0:T(8,128)(2,1)} %bitcast.70), calls=%async_computation | async-start | bytes 1048576 | tf_op jit(solution)/shard_map/all_to_all | solution.py:150
  9.9 40.2 %collective-permute-start = (bf16[16,128,128]{2,1,0:T(8,128)(2,1)S(1)}, bf16[16,128,128]{2,1,0:T(8,128)(2,1)S(1)}, u32[]{:S(2)}, u32[]{:S(2)}) collective-permute-start(bf16[16,128,128]{2,1,0:T(8,128)(2,1)S(1)} %copy-done), channel_id=1, source_target_pairs={{16,48},{48,80},{80,112},{112,144},{144,176},{176,208},{208,240},{... | collective-permute-start | bytes 1572872 | tf_op jit(solution)/shard_map/ppermute | solution.py:154
  17.9 39.4 %collective-permute-start.1 = (bf16[16,128,128]{2,1,0:T(8,128)(2,1)S(1)}, bf16[16,128,128]{2,1,0:T(8,128)(2,1)S(1)}, u32[]{:S(2)}, u32[]{:S(2)}) collective-permute-start(bf16[16,128,128]{2,1,0:T(8,128)(2,1)S(1)} %copy-done), channel_id=1, source_target_pairs={{0,16},{32,48},{64,80},{96,112},{128,144},{160,176},{192,208},{224... | collective-permute-start | bytes 1572872 | tf_op jit(solution)/shard_map/ppermute | solution.py:155
  20.0 17.3 %copy-start.7 = (bf16[128,8,4,128]{3,2,1,0:T(4,128)(2,1)S(1)}, bf16[128,8,4,128]{3,2,1,0:T(4,128)(2,1)}, u32[]{:S(2)}) copy-start(bf16[128,8,4,128]{3,2,1,0:T(4,128)(2,1)} %param.5) | copy-start | bytes 3145732
  27.1 0.8 copy-start.6
  30.8 35.5 %all-to-all-start.1 = ((bf16[32,64,128]{2,1,0:T(8,128)(2,1)}), bf16[32,64,128]{2,1,0:T(8,128)(2,1)S(1)}, u32[]{:S(2)}, u32[]{:S(2)}) async-start(bf16[32,64,128]{2,1,0:T(8,128)(2,1)} %pick_rows.1), calls=%async_computation.1 | async-start | bytes 1048576 | tf_op jit(solution)/shard_map/all_to_all | solution.py:164
  41.4 15.9 %collective-permute-start.3 = (bf16[1,128,1024]{2,1,0:T(8,128)(2,1)}, bf16[1,128,1024]{2,1,0:T(8,128)(2,1)S(1)}, u32[]{:S(2)}, u32[]{:S(2)}) collective-permute-start(bf16[1,128,1024]{2,1,0:T(8,128)(2,1)} %constant_dynamic-slice_fusion.1), channel_id=1, source_target_pairs={{0,480},{32,0},{64,32},{96,64},{128,96},{160,128},{192,160},{224,1... | collective-permute-start | bytes 786440 | tf_op jit(solution)/shard_map/ppermute | solution.py:157
  50.1 7.2 %collective-permute-start.2 = (bf16[16,128,128]{2,1,0:T(8,128)(2,1)S(1)}, bf16[16,128,128]{2,1,0:T(8,128)(2,1)}, u32[]{:S(2)}, u32[]{:S(2)}) collective-permute-start(bf16[16,128,128]{2,1,0:T(8,128)(2,1)S(1)} %collective-permute-done.refs_1_), channel_id=1, source_target_pairs={{16,0},{48,32},{80,64},{112,96},{144,128},{176,160},{208,192},{240... | collective-permute-start | bytes 1572872 | tf_op jit(solution)/shard_map/ppermute | solution.py:165
  56.5 0.7 copy-start.4
  57.3 9.0 %copy-start.1 = (s32[4,1]{1,0:T(4,128)S(1)}, s32[4,1]{1,0:T(4,128)}, u32[]{:S(2)}) copy-start(s32[4,1]{1,0:T(4,128)} %constant.62.clone.1.job_ref) | copy-start | bytes 52
  57.3 1.0 copy-start.5
  65.4 0.9 copy-start.2
  66.3 1.1 copy-start.3
  72.0 19.2 %copy-start.8 = (f32[4096]{0:T(1024)S(1)}, f32[4096]{0:T(1024)}, u32[]{:S(2)}) copy-start(f32[4096]{0:T(1024)} %param.7) | copy-start | bytes 49156
  72.0 46.6 %all-to-all-start.2 = ((bf16[16,8,4096]{2,1,0:T(8,128)(2,1)}), bf16[16,8,4096]{2,1,0:T(8,128)(2,1)S(1)}, u32[]{:S(2)}, u32[]{:S(2)}) async-start(bf16[16,8,4096]{2,1,0:T(8,128)(2,1)} %bitcast.14), calls=%async_computation.2 | async-start | bytes 2097152 | tf_op jit(solution)/shard_map/all_to_all | solution.py:184
  92.2 37.0 %copy-start.10 = (f32[8]{0:T(128)S(1)}, f32[8]{0:T(128)}, u32[]{:S(2)}) copy-start(f32[8]{0:T(128)} %param.8) | copy-start | bytes 100
  118.8 10.4 %collective-permute-start.4 = (f32[8,8,128]{2,1,0:T(8,128)S(1)}, f32[8,8,128]{2,1,0:T(8,128)S(1)}, u32[]{:S(2)}, u32[]{:S(2)}) collective-permute-start(f32[8,8,128]{2,1,0:T(8,128)S(1)} %get-tuple-element.16), channel_id=1, source_target_pairs={{0,32},{32,64},{64,96},{96,128},{128,160},{160,192},{192,224},{224... | collective-permute-start | bytes 98312 | tf_op jit(solution)/shard_map/ppermute | solution.py:189

commit v2 on v1

--- a/solution.py
+++ b/solution.py
@@ -37,78 +37,79 @@
     )(index, source)
 
 
-def ladder_kernel(tiles, amps, rows_from, cols_from, job_ref, *refs):
+def ladder_kernel(tiles, amps, job, rows_from, cols_from, job_ref, *refs):
     tile_refs, amp_refs = refs[:tiles], refs[tiles : tiles + amps]
     head_refs, (out_ref, *scratch) = refs[tiles + amps : -6], refs[-6:]
     own_ref, cols_ref, amp_ref, half_ref, total_ref = scratch
     aux, width = tile_refs[0].shape[0], tile_refs[0].shape[1]
     pairs, columns = half_ref.shape[0], total_ref.shape[0]
-    head = sum(ref.shape[1] for ref in head_refs)
-    jobs = (out_ref.shape[1] - head) // columns
-    for ref in head_refs:
-        out_ref[:, :head] = ref[...]
-
-    @pl.loop(0, jobs)
-    def _(job):
-        for number in rows_from:
-
-            @pl.when(job_ref[0, job] == number)
-            def _():
-                own_ref[...] = tile_refs[number][...]
-
-        for number in cols_from:
-
-            @pl.when(job_ref[1, job] == number)
-            def _():
-                for q in range(aux):
-                    cols_ref[q // QUAD, :, (q % QUAD) * width : (q % QUAD + 1) * width] = tile_refs[
-                        number
-                    ][q]
-
-        for number in range(amps):
-
-            @pl.when(job_ref[2, job] == number)
-            def _():
-                amp_ref[...] = amp_refs[number][job_ref[3, job]]
-
-        total_ref[...] = jnp.zeros_like(total_ref)
-
-        @pl.loop(0, aux // QUAD)
-        def _(step):
-            rows = own_ref[pl.ds(step * QUAD, QUAD)].reshape(QUAD * width, width)
-            for p in range(0, pairs, 2):
-                half = jnp.dot(
-                    rows,
-                    amp_ref[:, p * width : (p + 2) * width],
-                    preferred_element_type=jnp.float32,
-                ).astype(jnp.bfloat16)
-                for k in range(2):
-                    for q in range(QUAD):
-                        half_ref[p + k, :, q * width : (q + 1) * width] = half[
-                            q * width : (q + 1) * width, k * width : (k + 1) * width
-                        ]
-            total_ref[...] += lax.dot_general(
-                half_ref[...].reshape(pairs * width, QUAD * width),
-                cols_ref[step],
-                (((1,), (1,)), ((), ())),
+    head = out_ref.shape[1] - columns
+    for number, ref in enumerate(head_refs):
+        place = min(number, head // columns - 1) * columns
+
+        @pl.when(job_ref[job, 4] != number)
+        def _():
+            out_ref[:, place : place + columns] = ref[...]
+
+    for number in rows_from:
+
+        @pl.when(job_ref[job, 0] == number)
+        def _():
+            own_ref[...] = tile_refs[number][...]
+
+    for number in cols_from:
+
+        @pl.when(job_ref[job, 1] == number)
+        def _():
+            for q in range(aux):
+                cols_ref[q // QUAD, :, (q % QUAD) * width : (q % QUAD + 1) * width] = tile_refs[
+                    number
+                ][q]
+
+    for number in range(amps):
+
+        @pl.when(job_ref[job, 2] == number)
+        def _():
+            amp_ref[...] = amp_refs[number][job_ref[job, 3]]
+
+    total_ref[...] = jnp.zeros_like(total_ref)
+
+    @pl.loop(0, aux // QUAD)
+    def _(step):
+        rows = own_ref[pl.ds(step * QUAD, QUAD)].reshape(QUAD * width, width)
+        for p in range(0, pairs, 2):
+            half = jnp.dot(
+                rows,
+                amp_ref[:, p * width : (p + 2) * width],
                 preferred_element_type=jnp.float32,
-            )
-
-        for p in range(pairs):
-            start = pl.multiple_of(head + job * columns + p * width, width)
-            out_ref[:, pl.ds(start, width)] = total_ref[p * width : (p + 1) * width, :].astype(
-                jnp.bfloat16
-            )
-
-
-def partial_ladder(jobs, tiles, amps, heads, rows_from, cols_from):
+            ).astype(jnp.bfloat16)
+            for k in range(2):
+                for q in range(QUAD):
+                    half_ref[p + k, :, q * width : (q + 1) * width] = half[
+                        q * width : (q + 1) * width, k * width : (k + 1) * width
+                    ]
+        total_ref[...] += lax.dot_general(
+            half_ref[...].reshape(pairs * width, QUAD * width),
+            cols_ref[step],
+            (((1,), (1,)), ((), ())),
+            preferred_element_type=jnp.float32,
+        )
+
+    for p in range(pairs):
+        start = head + p * width
+        out_ref[:, start : start + width] = total_ref[p * width : (p + 1) * width, :].astype(
+            jnp.bfloat16
+        )
+
+
+def partial_ladder(jobs, job, tiles, amps, heads, rows_from, cols_from):
     aux, width, _ = tiles[0].shape
     columns = amps[0].shape[2]
-    pairs, count = columns // width, jobs.shape[1]
+    pairs = columns // width
     arrays = [*tiles, *amps, *heads]
-    total = sum(head.shape[1] for head in heads) + count * columns
+    total = max(len(heads), 1) * columns
     return pl.pallas_call(
-        functools.partial(ladder_kernel, len(tiles), len(amps), rows_from, cols_from),
+        functools.partial(ladder_kernel, len(tiles), len(amps), job, rows_from, cols_from),
         out_shape=jax.ShapeDtypeStruct((width, total), jnp.bfloat16),
         in_specs=[pl.BlockSpec(memory_space=pltpu.SMEM)]
         + [pl.BlockSpec(memory_space=pltpu.VMEM)] * len(arrays),
@@ -121,7 +122,7 @@
             pltpu.VMEM((columns, width), jnp.float32),
         ],
         cost_estimate=pl.CostEstimate(
-            flops=4 * count * aux * width * width * columns,
+            flops=4 * aux * width * width * columns,
             transcendentals=0,
             bytes_accessed=2 * sum(a.size for a in arrays) + 2 * width * total,
         ),
@@ -164,33 +165,37 @@
     far = lax.all_to_all(picked, "blk", 0, 0, tiled=True).reshape(integrals.shape)
     before = lax.ppermute(across, "blk", [(i, i - 1) for i in odd_tiles])
 
-    zero, one = jnp.int32(0), jnp.int32(1)
-
-    jobs = jnp.stack([zero, zero, zero, slot_of[0]]).reshape(4, 1)
-    piece = partial_ladder(jobs, [integrals], [amps], [], (0,), (0,))
-    jobs = jnp.stack(
-        [
-            jnp.stack([zero, 1 - odd]),
-            jnp.stack([3 - odd, odd]),
-            jnp.stack([zero, 1 - odd]),
-            jnp.stack([slot_of[1], odd * slot_of[2]]),
-        ]
-    ).astype(jnp.int32)
+    entry, row = jnp.arange(5)[None, :], jnp.arange(4)[:, None]
+    jobs = jnp.where(entry == 4, -1, 0)
+    for at, value in (
+        ((0, 3), slot_of[0]),
+        ((1, 0), 1 - odd),
+        ((1, 1), odd),
+        ((1, 2), 1 - odd),
+        ((1, 3), odd * slot_of[2]),
+        ((2, 1), 2 - odd),
+        ((2, 3), slot_of[1]),
+        ((3, 1), 1),
+        ((3, 3), near),
+        ((3, 4), 3 - odd),
+    ):
+        jobs = jnp.where((row == at[0]) & (entry == at[1]), value, jobs)
+    jobs = jobs.astype(jnp.int32)
+
+    same = partial_ladder(jobs, 0, [integrals], [amps], [], (0,), (0,))
+    cross = partial_ladder(jobs, 1, [integrals, across], [amps, amps_above], [], (0, 1), (0, 1))
+    handed = lax.ppermute(cross, "blk", [(i, (i + 2) % tiles) for i in even_tiles])
+    following = partial_ladder(jobs, 2, [integrals, beside, before], [amps], [], (0,), (1, 2))
     piece = partial_ladder(
-        jobs, [integrals, across, beside, before], [amps, amps_above], [piece], (0, 1), (0, 1, 2, 3)
-    )
-    jobs = jnp.stack([zero, one, zero, jnp.int32(near)]).reshape(4, 1)
-    piece = partial_ladder(jobs, [integrals, far], [amps], [piece], (0,), (1,))
+        jobs, 3, [integrals, far], [amps], [same, following, handed, cross], (0,), (1,)
+    )
     sums = lax.all_to_all(piece.reshape(groups, rows, -1), "grp", 0, 0, tiled=True)
     sums = jnp.sum(sums.astype(jnp.float32), axis=0).reshape(rows, slots, pairs, width)
     near_sum, far_sum = sums[:, :near], sums[:, near]
 
-    third = near_sum[:, 2]
-    carried = lax.ppermute(third, "blk", [(i, (i + 2) % tiles) for i in even_tiles])
-    third = jnp.where(odd == 1, third, carried)
     parts = [
         jnp.where(
-            own_offsets[s] == 0, near_sum[:, 0], jnp.where(own_offsets[s] == 1, near_sum[:, 1], third)
+            own_offsets[s] == 0, near_sum[:, 0], jnp.where(own_offsets[s] == 1, near_sum[:, 1], near_sum[:, 2])
         )
         for s in range(near)
     ]

time: 132 us -> 112 us (0.85)
  the two profiles are of different devices: /device:TPU:8 before, /device:TPU:6 now
where the time goes in v2:
time: 112 us; the launch traced here: 110 us
  starting transfers between devices  48.1 us (43%)
  waiting for transfers between devices  27 us (24%)
  Pallas kernels  19.2 us (17%)
  between operations  7.26 us (6%)
  local copies, waits for them, and re-layouts  5.26 us (5%)
  other arithmetic  3.27 us (3%)
    all_to_all x1, waiting for transfers between devices, local(): lax.all_to_all(piece.reshape(groups, rows, -1), 'grp', 0, 0, tiled=True)  19.2 us
    pallas_call x4, Pallas kernels, partial_ladder(): pl.pallas_call(functools.partial(ladder_kernel, len(tiles), len(amps), jo...  16.4 us
    all_to_all x1, starting transfers between devices, local(): lax.all_to_all(piece.reshape(groups, rows, -1), 'grp', 0, 0, tiled=True)  12.4 us
    all_to_all x1, starting transfers between devices, local(): lax.all_to_all(picked, 'blk', 0, 0, tiled=True).reshape(integrals.shape)  9.04 us
    all_to_all x1, waiting for transfers between devices, local(): lax.all_to_all(integrals.reshape(tiles, aux * width // tiles, width), 'bl...  7.33 us
    all_to_all x1, starting transfers between devices, local(): lax.all_to_all(integrals.reshape(tiles, aux * width // tiles, width), 'bl...  6.68 us
    ppermute x1, starting transfers between devices, local(): across = lax.ppermute(integrals, 'blk', hop)  6.56 us
    ppermute x1, starting transfers between devices, local(): lax.ppermute(lax.dynamic_slice_in_dim(amps, slot_of[2], 1, 0), 'blk', [(i...  5.76 us
  transfers between devices with their start and end apart: 8, of which 3 were waited for; matrix products, arithmetic and copies ran while one was open for 5% of the time, Pallas kernels for 13%

profile of v2, /device:TPU:6, one launch (start us, length us, event | category | flops | bytes accessed | tf_op | source)
XLA Modules:
  0.0 110.1 jit_solution(11823699616211033390)
XLA Ops:
  0.7 6.6 %collective-permute-start.1 = (bf16[16,128,128]{2,1,0:T(8,128)(2,1)}, bf16[16,128,128]{2,1,0:T(8,128)(2,1)}, u32[]{:S(2)}, u32[]{:S(2)}) collective-permute-start(bf16[16,128,128]{2,1,0:T(8,128)(2,1)} %refs_0_.7), channel_id=1, source_target_pairs={{16,48},{48,80},{80,112},{112,144},{144,176},{176,208},{208,240},{... | collective-permute-start | bytes 1572872 | tf_op jit(solution)/shard_map/ppermute | solution.py:155
  7.2 2.1 %collective-permute-start = (bf16[16,128,128]{2,1,0:T(8,128)(2,1)}, bf16[16,128,128]{2,1,0:T(8,128)(2,1)}, u32[]{:S(2)}, u32[]{:S(2)}) collective-permute-start(bf16[16,128,128]{2,1,0:T(8,128)(2,1)} %refs_0_.7), channel_id=1, source_target_pairs={{0,16},{32,48},{64,80},{96,112},{128,144},{160,176},{192,208},{224... | collective-permute-start | bytes 1572872 | tf_op jit(solution)/shard_map/ppermute | solution.py:156
  9.3 6.7 %all-to-all-start = ((bf16[32,64,128]{2,1,0:T(8,128)(2,1)}), bf16[32,64,128]{2,1,0:T(8,128)(2,1)S(1)}, u32[]{:S(2)}, u32[]{:S(2)}) async-start(bf16[32,64,128]{2,1,0:T(8,128)(2,1)} %bitcast.57), calls=%async_computation | async-start | bytes 1048576 | tf_op jit(solution)/shard_map/all_to_all | solution.py:151
  16.3 0.6 iota_reduce_fusion
  17.0 0.6 fusion.3
  20.1 5.8 %collective-permute-start.3 = (bf16[1,128,1024]{2,1,0:T(8,128)(2,1)S(1)}, bf16[1,128,1024]{2,1,0:T(8,128)(2,1)S(1)}, u32[]{:S(2)}, u32[]{:S(2)}) collective-permute-start(bf16[1,128,1024]{2,1,0:T(8,128)(2,1)S(1)} %constant_dynamic-slice_fusion.1), channel_id=1, source_target_pairs={{0,480},{32,0},{64,32},{96,64},{128,96},{160,128},{192,160},{224,1... | collective-permute-start | bytes 786440 | tf_op jit(solution)/shard_map/ppermute | solution.py:158
  25.9 0.5 and_select_fusion.1.index_ref
  26.5 7.3 %all-to-all-done.source_ref = bf16[32,64,128]{2,1,0:T(8,128)(2,1)S(1)} async-done(((bf16[32,64,128]{2,1,0:T(8,128)(2,1)}), bf16[32,64,128]{2,1,0:T(8,128)(2,1)S(1)}, u32[]{:S(2)}, u32[]{:S(2)}) %all-to-all-start) | async-done | bytes 524320 | tf_op jit(solution)/shard_map/all_to_all | solution.py:151
  33.8 0.8 copy-done.1
  34.6 2.8 %pick_rows.1 = bf16[32,64,128]{2,1,0:T(8,128)(2,1)} custom-call(s32[32]{0:T(128)} %and_select_fusion.1.index_ref, bf16[32,64,128]{2,1,0:T(8,128)(2,1)} %copy-done.1), custom_call_target="tpu_custom_call" | custom-call | bytes 1048576 | tf_op jit(solution)/shard_map/pick_rows/pallas_call | solution.py:26
  37.4 9.0 %all-to-all-start.1 = ((bf16[32,64,128]{2,1,0:T(8,128)(2,1)}), bf16[32,64,128]{2,1,0:T(8,128)(2,1)S(1)}, u32[]{:S(2)}, u32[]{:S(2)}) async-start(bf16[32,64,128]{2,1,0:T(8,128)(2,1)} %pick_rows.1), calls=%async_computation.1 | async-start | bytes 1048576 | tf_op jit(solution)/shard_map/all_to_all | solution.py:165
  46.5 1.3 %collective-permute-start.2 = (bf16[16,128,128]{2,1,0:T(8,128)(2,1)}, bf16[16,128,128]{2,1,0:T(8,128)(2,1)}, u32[]{:S(2)}, u32[]{:S(2)}) collective-permute-start(bf16[16,128,128]{2,1,0:T(8,128)(2,1)} %collective-permute-done.1.refs_1_), channel_id=1, source_target_pairs={{16,0},{48,32},{80,64},{112,96},{144,128},{176,160},{208,192},{240... | collective-permute-start | bytes 1572872 | tf_op jit(solution)/shard_map/ppermute | solution.py:166
  48.4 1.4 %select_select_fusion.job_ref = s32[4,5]{1,0:T(4,128)S(1)} fusion(s32[5]{0:T(128)S(1)} %broadcast_select_fusion, s32[]{:T(128)} %bitcast.3, s32[]{:T(128)S(6)} %select_n.179, s32[]{:T(128)S(6)} %sub.44, s32[]{:T(128)S(6)} %mul.9, s32[]{:T(128)S(6)} %sub.43, s32[]{:T(128)} %bitcast.1, s32[]{:T(128)S(6)} %sub.42, pred[5]{0:T(512)(128)(4,1)S(1)} %get-tuple-element.23, ...), kind=kLoop, calls=%fused_computation.19 | loop fusion | flops 400 | bytes 169 | tf_op jit(solution)/shard_map/jit(_where)/select_n | solution.py:182
  49.8 4.1 %shard_map.70.refs_6_ = bf16[128,1024]{1,0:T(8,128)(2,1)S(1)} custom-call(s32[4,5]{1,0:T(4,128)S(1)} %select_select_fusion.job_ref, bf16[16,128,128]{2,1,0:T(8,128)(2,1)S(1)} %copy-done, bf16[16,128,128]{2,1,0:T(8,128)(2,1)} %collective-permute-done.1.refs_1_, bf16[4,128,1024]{2,1,0:T(8,128)(2,1)S(1)} %reshape.234.refs_1_.refs_3_.refs_2_, ...), custom_call_target="tpu_custom_call" | custom-call | flops 1073741824 | bytes 2621440 | tf_op jit(solution)/shard_map/pallas_call | solution.py:111
  53.9 4.3 %collective-permute-start.4 = (bf16[128,1024]{1,0:T(8,128)(2,1)S(1)}, bf16[128,1024]{1,0:T(8,128)(2,1)S(1)}, u32[]{:S(2)}, u32[]{:S(2)}) collective-permute-start(bf16[128,1024]{1,0:T(8,128)(2,1)S(1)} %shard_map.70.refs_6_), channel_id=1, source_target_pairs={{0,32},{32,64},{64,96},{96,128},{128,160},{160,192},{192,224},{224... | collective-permute-start | bytes 786440 | tf_op jit(solution)/shard_map/ppermute | solution.py:187
  58.2 3.6 %shard_map.68.refs_3_ = bf16[128,1024]{1,0:T(8,128)(2,1)S(1)} custom-call(s32[4,5]{1,0:T(4,128)S(1)} %select_select_fusion.job_ref, bf16[16,128,128]{2,1,0:T(8,128)(2,1)S(1)} %copy-done, bf16[4,128,1024]{2,1,0:T(8,128)(2,1)S(1)} %reshape.234.refs_1_.refs_3_.refs_2_), custom_call_target="tpu_custom_call" | custom-call | flops 1073741824 | bytes 1835008 | tf_op jit(solution)/shard_map/pallas_call | solution.py:111
  61.8 4.2 %shard_map.69.refs_4_ = bf16[128,1024]{1,0:T(8,128)(2,1)S(1)} custom-call(s32[4,5]{1,0:T(4,128)S(1)} %select_select_fusion.job_ref, bf16[16,128,128]{2,1,0:T(8,128)(2,1)S(1)} %copy-done, bf16[16,128,128]{2,1,0:T(8,128)(2,1)} %collective-permute-done.refs_1_, bf16[16,128,128]{2,1,0:T(8,128)(2,1)} %collective-permute-done.2.refs_2_, ...), custom_call_target="tpu_custom_call" | custom-call | flops 1073741824 | bytes 2883584 | tf_op jit(solution)/shard_map/pallas_call | solution.py:111
  66.4 4.6 %shard_map.71 = bf16[128,4096]{1,0:T(8,128)(2,1)} custom-call(s32[4,5]{1,0:T(4,128)S(1)} %select_select_fusion.job_ref, bf16[16,128,128]{2,1,0:T(8,128)(2,1)S(1)} %copy-done, bf16[16,128,128]{2,1,0:T(8,128)(2,1)S(1)} %bitcast.58, bf16[4,128,1024]{2,1,0:T(8,128)(2,1)S(1)} %reshape.234.refs_1_.refs_3_.refs_2_, bf16[128,1024]{1,0:T(8,128)(2,1)S(1)} %shard_map.68.refs_3_, ...), custom_call_target="tpu_custom_call" | custom-call | flops 1073741824 | bytes 4194304 | tf_op jit(solution)/shard_map/pallas_call | solution.py:111
  71.0 12.4 %all-to-all-start.2 = ((bf16[16,8,4096]{2,1,0:T(8,128)(2,1)}), bf16[16,8,4096]{2,1,0:T(8,128)(2,1)S(1)}, u32[]{:S(2)}, u32[]{:S(2)}) async-start(bf16[16,8,4096]{2,1,0:T(8,128)(2,1)} %bitcast.8), calls=%async_computation.2 | async-start | bytes 2097152 | tf_op jit(solution)/shard_map/all_to_all | solution.py:192
  83.4 0.6 fusion.2
  87.9 0.9 constant_dynamic-slice_fusion
  89.1 19.2 %all-to-all-done.2 = bf16[16,8,4096]{2,1,0:T(8,128)(2,1)S(1)} async-done(((bf16[16,8,4096]{2,1,0:T(8,128)(2,1)}), bf16[16,8,4096]{2,1,0:T(8,128)(2,1)S(1)}, u32[]{:S(2)}, u32[]{:S(2)}) %all-to-all-start.2) | async-done | bytes 1048608 | tf_op jit(solution)/shard_map/all_to_all | solution.py:192
  108.6 0.7 copy.23
  109.3 0.7 copy.24
  (38 shorter events, 2.1 us)
Async XLA Ops:
  0.6 15.4 %copy-start.4 = (s32[32,4]{0,1:T(4,128)S(1)}, s32[32,4]{0,1:T(4,128)}, u32[]{:S(2)}) copy-start(s32[32,4]{0,1:T(4,128)} %param.9) | copy-start | bytes 1540
  0.6 18.2 %copy-start.2 = (bf16[128,8,4,128]{3,2,1,0:T(4,128)(2,1)S(1)}, bf16[128,8,4,128]{3,2,1,0:T(4,128)(2,1)}, u32[]{:S(2)}) copy-start(bf16[128,8,4,128]{3,2,1,0:T(4,128)(2,1)} %param.5) | copy-start | bytes 3145732
  0.7 45.8 %collective-permute-start.1 = (bf16[16,128,128]{2,1,0:T(8,128)(2,1)}, bf16[16,128,128]{2,1,0:T(8,128)(2,1)}, u32[]{:S(2)}, u32[]{:S(2)}) collective-permute-start(bf16[16,128,128]{2,1,0:T(8,128)(2,1)} %refs_0_.7), channel_id=1, source_target_pairs={{16,48},{48,80},{80,112},{112,144},{144,176},{176,208},{208,240},{... | collective-permute-start | bytes 1572872 | tf_op jit(solution)/shard_map/ppermute | solution.py:155
  7.2 54.5 %collective-permute-start = (bf16[16,128,128]{2,1,0:T(8,128)(2,1)}, bf16[16,128,128]{2,1,0:T(8,128)(2,1)}, u32[]{:S(2)}, u32[]{:S(2)}) collective-permute-start(bf16[16,128,128]{2,1,0:T(8,128)(2,1)} %refs_0_.7), channel_id=1, source_target_pairs={{0,16},{32,48},{64,80},{96,112},{128,144},{160,176},{192,208},{224... | collective-permute-start | bytes 1572872 | tf_op jit(solution)/shard_map/ppermute | solution.py:156
  9.3 24.5 %all-to-all-start = ((bf16[32,64,128]{2,1,0:T(8,128)(2,1)}), bf16[32,64,128]{2,1,0:T(8,128)(2,1)S(1)}, u32[]{:S(2)}, u32[]{:S(2)}) async-start(bf16[32,64,128]{2,1,0:T(8,128)(2,1)} %bitcast.57), calls=%async_computation | async-start | bytes 1048576 | tf_op jit(solution)/shard_map/all_to_all | solution.py:151
  20.1 29.7 %collective-permute-start.3 = (bf16[1,128,1024]{2,1,0:T(8,128)(2,1)S(1)}, bf16[1,128,1024]{2,1,0:T(8,128)(2,1)S(1)}, u32[]{:S(2)}, u32[]{:S(2)}) collective-permute-start(bf16[1,128,1024]{2,1,0:T(8,128)(2,1)S(1)} %constant_dynamic-slice_fusion.1), channel_id=1, source_target_pairs={{0,480},{32,0},{64,32},{96,64},{128,96},{160,128},{192,160},{224,1... | collective-permute-start | bytes 786440 | tf_op jit(solution)/shard_map/ppermute | solution.py:158
  26.5 23.3 %copy-start = (bf16[16,128,128]{2,1,0:T(8,128)(2,1)S(1)}, bf16[16,128,128]{2,1,0:T(8,128)(2,1)}, u32[]{:S(2)}) copy-start(bf16[16,128,128]{2,1,0:T(8,128)(2,1)} %refs_0_.7) | copy-start | bytes 1572868
  33.8 0.8 copy-start.1
  37.4 29.0 %all-to-all-start.1 = ((bf16[32,64,128]{2,1,0:T(8,128)(2,1)}), bf16[32,64,128]{2,1,0:T(8,128)(2,1)S(1)}, u32[]{:S(2)}, u32[]{:S(2)}) async-start(bf16[32,64,128]{2,1,0:T(8,128)(2,1)} %pick_rows.1), calls=%async_computation.1 | async-start | bytes 1048576 | tf_op jit(solution)/shard_map/all_to_all | solution.py:165
  46.5 15.3 %collective-permute-start.2 = (bf16[16,128,128]{2,1,0:T(8,128)(2,1)}, bf16[16,128,128]{2,1,0:T(8,128)(2,1)}, u32[]{:S(2)}, u32[]{:S(2)}) collective-permute-start(bf16[16,128,128]{2,1,0:T(8,128)(2,1)} %collective-permute-done.1.refs_1_), channel_id=1, source_target_pairs={{16,0},{48,32},{80,64},{112,96},{144,128},{176,160},{208,192},{240... | collective-permute-start | bytes 1572872 | tf_op jit(solution)/shard_map/ppermute | solution.py:166
  53.9 12.5 %collective-permute-start.4 = (bf16[128,1024]{1,0:T(8,128)(2,1)S(1)}, bf16[128,1024]{1,0:T(8,128)(2,1)S(1)}, u32[]{:S(2)}, u32[]{:S(2)}) collective-permute-start(bf16[128,1024]{1,0:T(8,128)(2,1)S(1)} %shard_map.70.refs_6_), channel_id=1, source_target_pairs={{0,32},{32,64},{64,96},{96,128},{128,160},{160,192},{192,224},{224... | collective-permute-start | bytes 786440 | tf_op jit(solution)/shard_map/ppermute | solution.py:187
  71.0 16.8 %copy-start.3 = (f32[4096]{0:T(1024)S(1)}, f32[4096]{0:T(1024)}, u32[]{:S(2)}) copy-start(f32[4096]{0:T(1024)} %param.7) | copy-start | bytes 49156
  71.0 37.2 %all-to-all-start.2 = ((bf16[16,8,4096]{2,1,0:T(8,128)(2,1)}), bf16[16,8,4096]{2,1,0:T(8,128)(2,1)S(1)}, u32[]{:S(2)}, u32[]{:S(2)}) async-start(bf16[16,8,4096]{2,1,0:T(8,128)(2,1)} %bitcast.8), calls=%async_computation.2 | async-start | bytes 2097152 | tf_op jit(solution)/shard_map/all_to_all | solution.py:192
  83.4 25.1 %copy-start.5 = (f32[8]{0:T(128)S(1)}, f32[8]{0:T(128)}, u32[]{:S(2)}) copy-start(f32[8]{0:T(128)} %param.8) | copy-start | bytes 100

commit v3 on v2

--- a/solution.py
+++ b/solution.py
@@ -9,17 +9,14 @@
 
 
 QUAD = 4
-
-
-def pick_kernel(index_ref, source_ref, out_ref, sem):
-    def copy(row):
-        return pltpu.make_async_copy(source_ref.at[index_ref[row]], out_ref.at[row], sem.at[row])
-
-    rows = out_ref.shape[0]
-    for row in range(rows):
-        copy(row).start()
-    for row in range(rows):
-        copy(row).wait()
+JOBS = (0, 0, 0, 0, -1, 1, 0, 1, 0, -1, 0, 2, 0, 0, -1, 0, 1, 0, 3, 3)
+PARITY = (0, 0, 0, 0, 0, -1, 1, -1, 0, 0, 0, -1, 0, 0, 0, 0, 0, 0, 0, -1)
+SLOT = (-1, -1, -1, 0, -1, -1, -1, -1, 2, -1, -1, -1, -1, 1, -1, -1, -1, -1, -1, -1)
+
+
+def pick_kernel(index_ref, source_ref, out_ref):
+    for row in range(out_ref.shape[0]):
+        out_ref[row] = source_ref[index_ref[row]]
 
 
 def pick_rows(source, index):
@@ -28,10 +25,9 @@
         out_shape=jax.ShapeDtypeStruct(source.shape, source.dtype),
         in_specs=[
             pl.BlockSpec(memory_space=pltpu.SMEM),
-            pl.BlockSpec(memory_space=pl.ANY),
+            pl.BlockSpec(memory_space=pltpu.VMEM),
         ],
         out_specs=pl.BlockSpec(memory_space=pltpu.VMEM),
-        scratch_shapes=[pltpu.SemaphoreType.DMA((source.shape[0],))],
         cost_estimate=pl.CostEstimate(flops=0, transcendentals=0, bytes_accessed=4 * source.size),
         name="pick_rows",
     )(index, source)
@@ -165,21 +161,14 @@
     far = lax.all_to_all(picked, "blk", 0, 0, tiled=True).reshape(integrals.shape)
     before = lax.ppermute(across, "blk", [(i, i - 1) for i in odd_tiles])
 
-    entry, row = jnp.arange(5)[None, :], jnp.arange(4)[:, None]
-    jobs = jnp.where(entry == 4, -1, 0)
-    for at, value in (
-        ((0, 3), slot_of[0]),
-        ((1, 0), 1 - odd),
-        ((1, 1), odd),
-        ((1, 2), 1 - odd),
-        ((1, 3), odd * slot_of[2]),
-        ((2, 1), 2 - odd),
-        ((2, 3), slot_of[1]),
-        ((3, 1), 1),
-        ((3, 3), near),
-        ((3, 4), 3 - odd),
-    ):
-        jobs = jnp.where((row == at[0]) & (entry == at[1]), value, jobs)
+    base = jnp.array(JOBS, jnp.int32).reshape(4, 5)
+    flags = jnp.array(PARITY, jnp.int32).reshape(4, 5)
+    slot = jnp.array(SLOT, jnp.int32).reshape(4, 5)
+    jobs = base + flags * odd
+    for number in range(near):
+        jobs = jobs + jnp.where(
+            (slot == number) & ((number < near - 1) | (odd == 1)), slot_of[number], 0
+        )
     jobs = jobs.astype(jnp.int32)
 
     same = partial_ladder(jobs, 0, [integrals], [amps], [], (0,), (0,))

time: 112 us -> 118 us (1.054)
  the two profiles are of different devices: /device:TPU:6 before, /device:TPU:8 now
where the time goes in v3:
time: 118 us; the launch traced here: 117 us
  starting transfers between devices  52.4 us (44%)
  waiting for transfers between devices  30.4 us (26%)
  Pallas kernels  18.3 us (16%)
  between operations  6.77 us (6%)
  local copies, waits for them, and re-layouts  5.29 us (4%)
  other arithmetic  3.78 us (3%)
    all_to_all x1, waiting for transfers between devices, local(): lax.all_to_all(piece.reshape(groups, rows, -1), 'grp', 0, 0, tiled=True)  16.6 us
    pallas_call x4, Pallas kernels, partial_ladder(): pl.pallas_call(functools.partial(ladder_kernel, len(tiles), len(amps), jo...  16.4 us
    all_to_all x1, starting transfers between devices, local(): lax.all_to_all(piece.reshape(groups, rows, -1), 'grp', 0, 0, tiled=True)  16 us
    all_to_all x1, starting transfers between devices, local(): lax.all_to_all(integrals.reshape(tiles, aux * width // tiles, width), 'bl...  9.2 us
    ppermute x1, starting transfers between devices, local(): across = lax.ppermute(integrals, 'blk', hop)  8 us
    ppermute x1, starting transfers between devices, local(): lax.ppermute(lax.dynamic_slice_in_dim(amps, slot_of[2], 1, 0), 'blk', [(i...  8 us
    all_to_all x1, waiting for transfers between devices, local(): lax.all_to_all(integrals.reshape(tiles, aux * width // tiles, width), 'bl...  6.33 us
    ppermute x1, waiting for transfers between devices, local(): lax.ppermute(lax.dynamic_slice_in_dim(amps, slot_of[2], 1, 0), 'blk', [(i...  3.98 us
  transfers between devices with their start and end apart: 8, of which 4 were waited for; matrix products, arithmetic and copies ran while one was open for 6% of the time, Pallas kernels for 12%

profile of v3, /device:TPU:8, one launch (start us, length us, event | category | flops | bytes accessed | tf_op | source)
XLA Modules:
  0.0 117.0 jit_solution(13539127171850996793)
XLA Ops:
  0.6 9.2 %all-to-all-start = ((bf16[32,64,128]{2,1,0:T(8,128)(2,1)}), bf16[32,64,128]{2,1,0:T(8,128)(2,1)S(1)}, u32[]{:S(2)}, u32[]{:S(2)}) async-start(bf16[32,64,128]{2,1,0:T(8,128)(2,1)} %bitcast.57), calls=%async_computation | async-start | bytes 1048576 | tf_op jit(solution)/shard_map/all_to_all | solution.py:147
  9.9 8.0 %collective-permute-start.1 = (bf16[16,128,128]{2,1,0:T(8,128)(2,1)S(1)}, bf16[16,128,128]{2,1,0:T(8,128)(2,1)}, u32[]{:S(2)}, u32[]{:S(2)}) collective-permute-start(bf16[16,128,128]{2,1,0:T(8,128)(2,1)S(1)} %copy-done), channel_id=1, source_target_pairs={{16,48},{48,80},{80,112},{112,144},{144,176},{176,208},{208,240},{... | collective-permute-start | bytes 1572872 | tf_op jit(solution)/shard_map/ppermute | solution.py:151
  17.9 2.1 %collective-permute-start = (bf16[16,128,128]{2,1,0:T(8,128)(2,1)S(1)}, bf16[16,128,128]{2,1,0:T(8,128)(2,1)}, u32[]{:S(2)}, u32[]{:S(2)}) collective-permute-start(bf16[16,128,128]{2,1,0:T(8,128)(2,1)S(1)} %copy-done), channel_id=1, source_target_pairs={{0,16},{32,48},{64,80},{96,112},{128,144},{160,176},{192,208},{224... | collective-permute-start | bytes 1572872 | tf_op jit(solution)/shard_map/ppermute | solution.py:152
  20.8 6.3 %all-to-all-done.source_ref = bf16[32,64,128]{2,1,0:T(8,128)(2,1)S(1)} async-done(((bf16[32,64,128]{2,1,0:T(8,128)(2,1)}), bf16[32,64,128]{2,1,0:T(8,128)(2,1)S(1)}, u32[]{:S(2)}, u32[]{:S(2)}) %all-to-all-start) | async-done | bytes 524320 | tf_op jit(solution)/shard_map/all_to_all | solution.py:147
  27.1 0.8 copy-done.1
  27.9 1.9 %pick_rows.1 = bf16[32,64,128]{2,1,0:T(8,128)(2,1)} custom-call(s32[32]{0:T(128)} %and_select_fusion.1.index_ref, bf16[32,64,128]{2,1,0:T(8,128)(2,1)} %copy-done.1), custom_call_target="tpu_custom_call" | custom-call | bytes 1048576 | tf_op jit(solution)/shard_map/pick_rows/pallas_call | solution.py:23
  29.8 3.9 %all-to-all-start.1 = ((bf16[32,64,128]{2,1,0:T(8,128)(2,1)}), bf16[32,64,128]{2,1,0:T(8,128)(2,1)S(1)}, u32[]{:S(2)}, u32[]{:S(2)}) async-start(bf16[32,64,128]{2,1,0:T(8,128)(2,1)} %pick_rows.1), calls=%async_computation.1 | async-start | bytes 1048576 | tf_op jit(solution)/shard_map/all_to_all | solution.py:161
  33.7 0.6 iota_reduce_fusion
  34.3 0.6 fusion.5
  37.6 8.0 %collective-permute-start.3 = (bf16[1,128,1024]{2,1,0:T(8,128)(2,1)S(1)}, bf16[1,128,1024]{2,1,0:T(8,128)(2,1)S(1)}, u32[]{:S(2)}, u32[]{:S(2)}) collective-permute-start(bf16[1,128,1024]{2,1,0:T(8,128)(2,1)S(1)} %constant_dynamic-slice_fusion.1), channel_id=1, source_target_pairs={{0,480},{32,0},{64,32},{96,64},{128,96},{160,128},{192,160},{224,1... | collective-permute-start | bytes 786440 | tf_op jit(solution)/shard_map/ppermute | solution.py:154
  45.6 1.3 %collective-permute-start.2 = (bf16[16,128,128]{2,1,0:T(8,128)(2,1)}, bf16[16,128,128]{2,1,0:T(8,128)(2,1)}, u32[]{:S(2)}, u32[]{:S(2)}) collective-permute-start(bf16[16,128,128]{2,1,0:T(8,128)(2,1)} %collective-permute-done.1.refs_1_), channel_id=1, source_target_pairs={{16,0},{48,32},{80,64},{112,96},{144,128},{176,160},{208,192},{240... | collective-permute-start | bytes 1572872 | tf_op jit(solution)/shard_map/ppermute | solution.py:162
  47.0 1.9 %fusion = s32[20]{0:T(128)S(1)} fusion(pred[20]{0:T(512)(128)(4,1)S(1)} %copy-done.10, pred[]{:T(512)S(6)} %eq.101, s32[20]{0:T(128)S(1)} %copy-done.6, pred[20]{0:T(512)(128)(4,1)S(1)} %copy-done.9, pred[20]{0:T(512)(128)(4,1)S(1)} %copy-done.8, s32[20]{0:T(128)S(1)} %copy-done.7, s32[]{:T(128)} %bitcast.3, s32[]{:T(128)} %bitcast.2, s32[]{:T(128)} %bitcast.1, ...), kind=kLoop, calls=%fused_computation.28 | loop fusion | flops 180 | bytes 317 | tf_op jit(solution)/shard_map/add | solution.py:169
  49.0 4.0 %collective-permute-done.3.refs_3_ = bf16[1,128,1024]{2,1,0:T(8,128)(2,1)S(1)} collective-permute-done((bf16[1,128,1024]{2,1,0:T(8,128)(2,1)S(1)}, bf16[1,128,1024]{2,1,0:T(8,128)(2,1)S(1)}, u32[]{:S(2)}, u32[]{:S(2)}) %collective-permute-start.3) | collective-permute-done | bytes 262176 | tf_op jit(solution)/shard_map/ppermute | solution.py:154
  53.0 4.1 %shard_map.97.refs_6_ = bf16[128,1024]{1,0:T(8,128)(2,1)S(1)} custom-call(s32[4,5]{1,0:T(4,128)S(1)} %reshape.214.job_ref, bf16[16,128,128]{2,1,0:T(8,128)(2,1)S(1)} %copy-done, bf16[16,128,128]{2,1,0:T(8,128)(2,1)} %collective-permute-done.1.refs_1_, bf16[4,128,1024]{2,1,0:T(8,128)(2,1)S(1)} %reshape.211.refs_1_.refs_3_.refs_2_, ...), custom_call_target="tpu_custom_call" | custom-call | flops 1073741824 | bytes 2621440 | tf_op jit(solution)/shard_map/pallas_call | solution.py:107
  57.1 3.9 %collective-permute-start.4 = (bf16[128,1024]{1,0:T(8,128)(2,1)S(1)}, bf16[128,1024]{1,0:T(8,128)(2,1)S(1)}, u32[]{:S(2)}, u32[]{:S(2)}) collective-permute-start(bf16[128,1024]{1,0:T(8,128)(2,1)S(1)} %shard_map.97.refs_6_), channel_id=1, source_target_pairs={{0,32},{32,64},{64,96},{96,128},{128,160},{160,192},{192,224},{224... | collective-permute-start | bytes 786440 | tf_op jit(solution)/shard_map/ppermute | solution.py:176
  61.0 3.6 %shard_map.95.refs_3_ = bf16[128,1024]{1,0:T(8,128)(2,1)S(1)} custom-call(s32[4,5]{1,0:T(4,128)S(1)} %reshape.214.job_ref, bf16[16,128,128]{2,1,0:T(8,128)(2,1)S(1)} %copy-done, bf16[4,128,1024]{2,1,0:T(8,128)(2,1)S(1)} %reshape.211.refs_1_.refs_3_.refs_2_), custom_call_target="tpu_custom_call" | custom-call | flops 1073741824 | bytes 1835008 | tf_op jit(solution)/shard_map/pallas_call | solution.py:107
  64.5 4.2 %shard_map.96.refs_4_ = bf16[128,1024]{1,0:T(8,128)(2,1)S(1)} custom-call(s32[4,5]{1,0:T(4,128)S(1)} %reshape.214.job_ref, bf16[16,128,128]{2,1,0:T(8,128)(2,1)S(1)} %copy-done, bf16[16,128,128]{2,1,0:T(8,128)(2,1)} %collective-permute-done.refs_1_, bf16[16,128,128]{2,1,0:T(8,128)(2,1)} %collective-permute-done.2.refs_2_, ...), custom_call_target="tpu_custom_call" | custom-call | flops 1073741824 | bytes 2883584 | tf_op jit(solution)/shard_map/pallas_call | solution.py:107
  68.8 3.5 %collective-permute-done.4.refs_5_ = bf16[128,1024]{1,0:T(8,128)(2,1)S(1)} collective-permute-done((bf16[128,1024]{1,0:T(8,128)(2,1)S(1)}, bf16[128,1024]{1,0:T(8,128)(2,1)S(1)}, u32[]{:S(2)}, u32[]{:S(2)}) %collective-permute-start.4) | collective-permute-done | bytes 262176 | tf_op jit(solution)/shard_map/ppermute | solution.py:176
  72.3 4.6 %shard_map.98 = bf16[128,4096]{1,0:T(8,128)(2,1)} custom-call(s32[4,5]{1,0:T(4,128)S(1)} %reshape.214.job_ref, bf16[16,128,128]{2,1,0:T(8,128)(2,1)S(1)} %copy-done, bf16[16,128,128]{2,1,0:T(8,128)(2,1)S(1)} %bitcast.58, bf16[4,128,1024]{2,1,0:T(8,128)(2,1)S(1)} %reshape.211.refs_1_.refs_3_.refs_2_, bf16[128,1024]{1,0:T(8,128)(2,1)S(1)} %shard_map.95.refs_3_, ...), custom_call_target="tpu_custom_call" | custom-call | flops 1073741824 | bytes 4194304 | tf_op jit(solution)/shard_map/pallas_call | solution.py:107
  76.9 16.0 %all-to-all-start.2 = ((bf16[16,8,4096]{2,1,0:T(8,128)(2,1)}), bf16[16,8,4096]{2,1,0:T(8,128)(2,1)S(1)}, u32[]{:S(2)}, u32[]{:S(2)}) async-start(bf16[16,8,4096]{2,1,0:T(8,128)(2,1)} %bitcast.8), calls=%async_computation.2 | async-start | bytes 2097152 | tf_op jit(solution)/shard_map/all_to_all | solution.py:181
  97.4 0.9 constant_dynamic-slice_fusion
  98.6 16.6 %all-to-all-done.2 = bf16[16,8,4096]{2,1,0:T(8,128)(2,1)S(1)} async-done(((bf16[16,8,4096]{2,1,0:T(8,128)(2,1)}), bf16[16,8,4096]{2,1,0:T(8,128)(2,1)S(1)}, u32[]{:S(2)}, u32[]{:S(2)}) %all-to-all-start.2) | async-done | bytes 1048608 | tf_op jit(solution)/shard_map/all_to_all | solution.py:181
  115.5 0.7 copy.26
  116.2 0.7 copy.27
  (43 shorter events, 2.8 us)
Async XLA Ops:
  0.6 9.2 %copy-start = (bf16[16,128,128]{2,1,0:T(8,128)(2,1)S(1)}, bf16[16,128,128]{2,1,0:T(8,128)(2,1)}, u32[]{:S(2)}) copy-start(bf16[16,128,128]{2,1,0:T(8,128)(2,1)} %refs_0_.7) | copy-start | bytes 1572868
  0.6 19.3 %copy-start.4 = (s32[32,4]{0,1:T(4,128)S(1)}, s32[32,4]{0,1:T(4,128)}, u32[]{:S(2)}) copy-start(s32[32,4]{0,1:T(4,128)} %param.12) | copy-start | bytes 1540
  0.6 26.5 %all-to-all-start = ((bf16[32,64,128]{2,1,0:T(8,128)(2,1)}), bf16[32,64,128]{2,1,0:T(8,128)(2,1)S(1)}, u32[]{:S(2)}, u32[]{:S(2)}) async-start(bf16[32,64,128]{2,1,0:T(8,128)(2,1)} %bitcast.57), calls=%async_computation | async-start | bytes 1048576 | tf_op jit(solution)/shard_map/all_to_all | solution.py:147
  9.9 35.8 %collective-permute-start.1 = (bf16[16,128,128]{2,1,0:T(8,128)(2,1)S(1)}, bf16[16,128,128]{2,1,0:T(8,128)(2,1)}, u32[]{:S(2)}, u32[]{:S(2)}) collective-permute-start(bf16[16,128,128]{2,1,0:T(8,128)(2,1)S(1)} %copy-done), channel_id=1, source_target_pairs={{16,48},{48,80},{80,112},{112,144},{144,176},{176,208},{208,240},{... | collective-permute-start | bytes 1572872 | tf_op jit(solution)/shard_map/ppermute | solution.py:151
  17.9 46.6 %collective-permute-start = (bf16[16,128,128]{2,1,0:T(8,128)(2,1)S(1)}, bf16[16,128,128]{2,1,0:T(8,128)(2,1)}, u32[]{:S(2)}, u32[]{:S(2)}) collective-permute-start(bf16[16,128,128]{2,1,0:T(8,128)(2,1)S(1)} %copy-done), channel_id=1, source_target_pairs={{0,16},{32,48},{64,80},{96,112},{128,144},{160,176},{192,208},{224... | collective-permute-start | bytes 1572872 | tf_op jit(solution)/shard_map/ppermute | solution.py:152
  20.8 15.4 %copy-start.2 = (bf16[128,8,4,128]{3,2,1,0:T(4,128)(2,1)S(1)}, bf16[128,8,4,128]{3,2,1,0:T(4,128)(2,1)}, u32[]{:S(2)}) copy-start(bf16[128,8,4,128]{3,2,1,0:T(4,128)(2,1)} %param.8) | copy-start | bytes 3145732
  27.1 0.8 copy-start.1
  29.8 42.5 %all-to-all-start.1 = ((bf16[32,64,128]{2,1,0:T(8,128)(2,1)}), bf16[32,64,128]{2,1,0:T(8,128)(2,1)S(1)}, u32[]{:S(2)}, u32[]{:S(2)}) async-start(bf16[32,64,128]{2,1,0:T(8,128)(2,1)} %pick_rows.1), calls=%async_computation.1 | async-start | bytes 1048576 | tf_op jit(solution)/shard_map/all_to_all | solution.py:161
  36.4 10.6 %copy-start.6 = (s32[20]{0:T(128)S(1)}, s32[20]{0:T(128)}, u32[]{:S(2)}) copy-start(s32[20]{0:T(128)} %constant.78.clone) | copy-start | bytes 244
  36.4 10.6 %copy-start.7 = (s32[20]{0:T(128)S(1)}, s32[20]{0:T(128)}, u32[]{:S(2)}) copy-start(s32[20]{0:T(128)} %constant.79.clone) | copy-start | bytes 244
  36.4 10.6 %copy-start.8 = (pred[20]{0:T(512)(128)(4,1)S(1)}, pred[20]{0:T(512)(128)(4,1)}, u32[]{:S(2)}) copy-start(pred[20]{0:T(512)(128)(4,1)} %constant.81) | copy-start | bytes 64
  36.4 10.6 %copy-start.9 = (pred[20]{0:T(512)(128)(4,1)S(1)}, pred[20]{0:T(512)(128)(4,1)}, u32[]{:S(2)}) copy-start(pred[20]{0:T(512)(128)(4,1)} %constant.82) | copy-start | bytes 64
  36.4 10.6 %copy-start.10 = (pred[20]{0:T(512)(128)(4,1)S(1)}, pred[20]{0:T(512)(128)(4,1)}, u32[]{:S(2)}) copy-start(pred[20]{0:T(512)(128)(4,1)} %constant.83) | copy-start | bytes 64
  37.6 15.4 %collective-permute-start.3 = (bf16[1,128,1024]{2,1,0:T(8,128)(2,1)S(1)}, bf16[1,128,1024]{2,1,0:T(8,128)(2,1)S(1)}, u32[]{:S(2)}, u32[]{:S(2)}) collective-permute-start(bf16[1,128,1024]{2,1,0:T(8,128)(2,1)S(1)} %constant_dynamic-slice_fusion.1), channel_id=1, source_target_pairs={{0,480},{32,0},{64,32},{96,64},{128,96},{160,128},{192,160},{224,1... | collective-permute-start | bytes 786440 | tf_op jit(solution)/shard_map/ppermute | solution.py:154
  45.6 18.9 %collective-permute-start.2 = (bf16[16,128,128]{2,1,0:T(8,128)(2,1)}, bf16[16,128,128]{2,1,0:T(8,128)(2,1)}, u32[]{:S(2)}, u32[]{:S(2)}) collective-permute-start(bf16[16,128,128]{2,1,0:T(8,128)(2,1)} %collective-permute-done.1.refs_1_), channel_id=1, source_target_pairs={{16,0},{48,32},{80,64},{112,96},{144,128},{176,160},{208,192},{240... | collective-permute-start | bytes 1572872 | tf_op jit(solution)/shard_map/ppermute | solution.py:162
  57.1 15.2 %collective-permute-start.4 = (bf16[128,1024]{1,0:T(8,128)(2,1)S(1)}, bf16[128,1024]{1,0:T(8,128)(2,1)S(1)}, u32[]{:S(2)}, u32[]{:S(2)}) collective-permute-start(bf16[128,1024]{1,0:T(8,128)(2,1)S(1)} %shard_map.97.refs_6_), channel_id=1, source_target_pairs={{0,32},{32,64},{64,96},{96,128},{128,160},{160,192},{192,224},{224... | collective-permute-start | bytes 786440 | tf_op jit(solution)/shard_map/ppermute | solution.py:176
  76.9 20.5 %copy-start.3 = (f32[4096]{0:T(1024)S(1)}, f32[4096]{0:T(1024)}, u32[]{:S(2)}) copy-start(f32[4096]{0:T(1024)} %param.10) | copy-start | bytes 49156
  76.9 38.3 %all-to-all-start.2 = ((bf16[16,8,4096]{2,1,0:T(8,128)(2,1)}), bf16[16,8,4096]{2,1,0:T(8,128)(2,1)S(1)}, u32[]{:S(2)}, u32[]{:S(2)}) async-start(bf16[16,8,4096]{2,1,0:T(8,128)(2,1)} %bitcast.8), calls=%async_computation.2 | async-start | bytes 2097152 | tf_op jit(solution)/shard_map/all_to_all | solution.py:181
  92.9 22.5 %copy-start.5 = (f32[8]{0:T(128)S(1)}, f32[8]{0:T(128)}, u32[]{:S(2)}) copy-start(f32[8]{0:T(128)} %param.11) | copy-start | bytes 100
